TPU v7x, 128 devices: a whole 4x4x4 slice. The times are simulated.
128 devices in a mesh: seq: 8 (over y_lo, x), samp: 16 (over y_hi, z, core).
Axes of the slice: x: 4, y: 4 (y_hi: 2, y_lo: 2; y = y_hi * 2 + y_lo), z: 4, core: 2. Of those that a mesh axis runs over, the one named last changes fastest.
Arguments:
- prompt_ids: int32 [2048], replicated, may hold values from 0 to 64127
- comp_ids: int32 [64, 2], replicated, may hold values from 0 to 64127
- prefix_len: int32 [1], replicated, may hold values from 8192 to 16384
- prompt_offset: int32 [1], replicated, may hold values from 16384 to 32768
- embed_table: bfloat16 [64128, 8192], P('seq', 'samp'), may hold values from -3 to 3
- attn_gain: bfloat16 [8192], P('samp'), may hold values from 0.099609375 to 1.8984375
- query_key_value_weight: bfloat16 [8192, 10240], P('samp', 'seq')
- w_out: bfloat16 [8192, 8192], P('seq', 'samp'), may hold values from -0.29882812 to 0.29882812
- key_value_cache: bfloat16 [2, 8, 16384, 128], P(None, 'seq'), may hold values from -6 to 6
Outputs:
- prompt_out: bfloat16 [2048, 8192], P('seq', 'samp')
- comp_out: bfloat16 [64, 2, 8192], P('seq', None, 'samp')
Inputs may be any that keep to these rules, and one draw needn't show every extreme that they name: The valid cache slots are slots 0 to prefix_len - 1. The valid cache slots hold the positions directly before prompt_offset.
All inputs are finite; a program needn't handle non-finite values.
Results may differ from a plain program's by a relative error of at most 0.03.
Values may be sent and summed in bfloat16 or wider, within the bound.
No kernel may reach another device: no remote copies, remote signals or barrier semaphores. Data moves between devices by JAX's collectives and lax.ppermute only.
A program may use at most 192 MiB of HBM per device.

v0:
```python
import math
import jax
import jax.numpy as jnp
from jax import lax
from jax.sharding import PartitionSpec as P

NORM_EPS = 1e-05
MASK_FILL = -1e30


def from_everyone(shard, axis):
    copies = jnp.broadcast_to(shard, (lax.axis_size(axis), *shard.shape))
    return lax.all_to_all(copies, axis, split_axis=0, concat_axis=0, tiled=True)


def of_everyone(shard, axis):
    return from_everyone(shard, axis).sum(axis=0)


def sent_together(arrays, axis, dim, along):
    both = jnp.concatenate(arrays, axis=along)
    filled, at, outs = (lax.all_gather(both, axis, axis=dim, tiled=True), 0, [])
    for a in arrays:
        outs.append(lax.slice_in_dim(filled, at, at + a.shape[along], axis=along))
        at += a.shape[along]
    return tuple(outs)


def in_blocks(shard, dim, length):
    shape = shard.shape
    parts = shard.reshape(*shape[:dim], length, shape[dim] // length, *shape[dim + 1 :])
    return jnp.moveaxis(parts, dim, 0)


def sent_and_summed(shard, axis, dim):
    length = lax.axis_size(axis)
    parts = lax.all_to_all(in_blocks(shard, dim, length), axis, 0, 0, tiled=True)
    return jnp.sum(parts.astype(jnp.float32), axis=0)


def rope_freqs(head_dim):
    half_dim = head_dim // 2
    dim_index = jnp.arange(half_dim, dtype=jnp.float32)
    base_freq = 1.0 / jnp.power(500000.0, 2.0 * dim_index / head_dim)
    wavelength = 2.0 * math.pi / base_freq
    blend = (8192.0 / wavelength - 1.0) / 3.0
    middle = (1.0 - blend) * base_freq / 8.0 + blend * base_freq
    return jnp.where(
        wavelength > 8192.0, base_freq / 8.0, jnp.where(wavelength < 2048.0, base_freq, middle)
    )


def rotate(vectors, positions):
    angles = positions[:, None] * rope_freqs(vectors.shape[-1])[None, :]
    bcast_shape = (angles.shape[0],) + (1,) * (vectors.ndim - 2) + (angles.shape[1],)
    cosine = jnp.cos(angles).reshape(bcast_shape)
    sine_vals = jnp.sin(angles).reshape(bcast_shape)
    half_dim = vectors.shape[-1] // 2
    first_half = vectors[..., :half_dim]
    second_half = vectors[..., half_dim:]
    return jnp.concatenate(
        [
            first_half * cosine - second_half * sine_vals,
            second_half * cosine + first_half * sine_vals,
        ],
        axis=-1,
    )


def absorb(running, queries, key_block, value_block, live_mask, key_form):
    run_max, run_sum, run_acc = running
    score_scale = 1.0 / math.sqrt(queries.shape[-1])
    scores = (
        jnp.einsum(
            "rgqd," + key_form + "->rgqk", queries, key_block, preferred_element_type=jnp.float32
        )
        * score_scale
    )
    live_wide = live_mask[:, None, None, :]
    scores = jnp.where(live_wide, scores, MASK_FILL)
    new_max = jnp.maximum(run_max, jnp.max(scores, axis=-1))
    weights = jnp.where(live_wide, jnp.exp(scores - new_max[..., None]), 0.0)
    factor = jnp.exp(run_max - new_max)
    run_sum = run_sum * factor + jnp.sum(weights, axis=-1)
    run_acc = run_acc * factor[..., None] + jnp.einsum(
        "rgqk," + key_form + "->rgqd",
        weights.astype(jnp.bfloat16),
        value_block,
        preferred_element_type=jnp.float32,
    )
    return (new_max, run_sum, run_acc)


def seq_order(row_block, samp_count, seq_count, own_prompt, own_comp):
    row_width = row_block.shape[1]
    blocks = row_block.reshape(samp_count, own_prompt + own_comp, row_width)
    prompt_part = blocks[:, :own_prompt].reshape(
        seq_count, samp_count * own_prompt // seq_count, row_width
    )
    comp_part = blocks[:, own_prompt:].reshape(
        seq_count, samp_count * own_comp // seq_count, row_width
    )
    return jnp.concatenate([prompt_part, comp_part], axis=1).reshape(-1, row_width)


def body(
    prompt_ids,
    comp_ids,
    prefix_len,
    prompt_offset,
    embed_table,
    attn_gain,
    query_key_value_weight,
    w_out,
    key_value_cache,
):
    seq_count = lax.axis_size("seq")
    samp_count = lax.axis_size("samp")
    seq_index = lax.axis_index("seq")
    samp_index = lax.axis_index("samp")
    prompt_len = prompt_ids.shape[0]
    comp_count, new_len = comp_ids.shape
    vocab_rows, local_width = embed_table.shape
    group_dev = key_value_cache.shape[1]
    cache_len = key_value_cache.shape[2]
    head_dim = key_value_cache.shape[3]
    columns = query_key_value_weight.shape[1]
    heads_per = columns // (group_dev * head_dim) - 2
    own_prompt = prompt_len // samp_count
    own_comp = comp_count * new_len // samp_count
    own_rows = own_prompt + own_comp
    arranged = jnp.concatenate(
        [prompt_ids.reshape(samp_count, own_prompt), comp_ids.reshape(samp_count, own_comp)], axis=1
    ).reshape(-1)
    local_ids = arranged - seq_index * vocab_rows
    inside = (local_ids >= 0) & (local_ids < vocab_rows)
    picked = jnp.take(embed_table, jnp.clip(local_ids, 0, vocab_rows - 1), axis=0)
    partial_rows = jnp.where(inside[:, None], picked, jnp.zeros((), jnp.bfloat16))
    embedded = lax.psum(partial_rows, "seq").astype(jnp.float32).astype(jnp.bfloat16)
    wide = embedded.astype(jnp.float32)
    square_sums = of_everyone(jnp.sum(wide * wide, axis=1), "samp")
    inv_rms = lax.rsqrt(square_sums / (local_width * samp_count) + NORM_EPS)
    normalized_rows = (wide * inv_rms[:, None] * attn_gain.astype(jnp.float32)[None, :]).astype(
        jnp.bfloat16
    )
    own_features = lax.all_to_all(normalized_rows, "samp", split_axis=0, concat_axis=1, tiled=True)
    projected_rows = jnp.dot(
        own_features,
        lax.all_gather(query_key_value_weight, "samp", axis=0, tiled=True),
        preferred_element_type=jnp.float32,
    )
    start_pos = prompt_offset[0]
    own_prompt_pos = start_pos + samp_index * own_prompt + jnp.arange(own_prompt, dtype=jnp.int32)
    own_comp_pos = start_pos + prompt_len + jnp.arange(own_comp, dtype=jnp.int32) % new_len
    own_pos = jnp.concatenate([own_prompt_pos, own_comp_pos]).astype(jnp.float32)
    shaped = projected_rows.reshape(own_rows, group_dev, heads_per + 2, head_dim)
    queries = rotate(shaped[:, :, :heads_per], own_pos).astype(jnp.bfloat16)
    key_rows = rotate(shaped[:, :, heads_per], own_pos).astype(jnp.bfloat16)
    value_rows = shaped[:, :, heads_per + 1].astype(jnp.bfloat16)
    running = (
        jnp.full((own_rows, group_dev, heads_per), MASK_FILL, jnp.float32),
        jnp.zeros((own_rows, group_dev, heads_per), jnp.float32),
        jnp.zeros((own_rows, group_dev, heads_per, head_dim), jnp.float32),
    )
    prefix_count = prefix_len[0]
    block_len = min(cache_len, 2048)

    def cache_step(block_index, running_in):
        first_slot = block_index * block_len
        cache_block = lax.dynamic_slice(
            key_value_cache, (0, 0, first_slot, 0), (2, group_dev, block_len, head_dim)
        )
        slot_ids = first_slot + jnp.arange(block_len, dtype=jnp.int32)
        live_mask = jnp.broadcast_to((slot_ids < prefix_count)[None, :], (own_rows, block_len))
        return absorb(running_in, queries, cache_block[0], cache_block[1], live_mask, "gkd")

    running = lax.fori_loop(0, cache_len // block_len, cache_step, running)
    row_ids = jnp.arange(own_rows, dtype=jnp.int32)
    comp_key_ids = jnp.arange(own_comp, dtype=jnp.int32)
    row_local = row_ids - own_prompt
    comp_live = (
        (row_ids[:, None] >= own_prompt)
        & (comp_key_ids[None, :] // new_len == row_local[:, None] // new_len)
        & (comp_key_ids[None, :] % new_len <= row_local[:, None] % new_len)
    )
    running = absorb(
        running, queries, key_rows[own_prompt:], value_rows[own_prompt:], comp_live, "kgd"
    )
    row_prompt = jnp.where(row_ids < own_prompt, samp_index * own_prompt + row_ids, prompt_len)
    piece_keys, piece_values = sent_together(
        (key_rows[:own_prompt], value_rows[:own_prompt]), "samp", 0, 1
    )
    key_pos = jnp.arange(piece_keys.shape[0], dtype=jnp.int32)
    live_mask = key_pos[None, :] <= row_prompt[:, None]
    running = absorb(running, queries, piece_keys, piece_values, live_mask, "kgd")
    run_max, run_sum, run_acc = running
    context = (
        (run_acc / run_sum[..., None])
        .astype(jnp.bfloat16)
        .reshape(own_rows, group_dev * heads_per * head_dim)
    )
    out_rows = prompt_len // seq_count + comp_count * new_len // seq_count
    terms = jnp.dot(
        lax.all_gather(context, "samp", axis=0, tiled=True),
        w_out,
        preferred_element_type=jnp.float32,
    )
    summed = sent_and_summed(
        seq_order(terms, samp_count, seq_count, own_prompt, own_comp).astype(jnp.bfloat16), "seq", 0
    )
    residual = lax.dynamic_slice_in_dim(
        seq_order(embedded, samp_count, seq_count, own_prompt, own_comp),
        seq_index * out_rows,
        out_rows,
        0,
    )
    total = summed + residual.astype(jnp.float32)
    prompt_rows = prompt_len // seq_count
    prompt_out = total[:prompt_rows].astype(jnp.bfloat16)
    comp_out = (
        total[prompt_rows:]
        .reshape(comp_count // seq_count, new_len, local_width)
        .astype(jnp.bfloat16)
    )
    return (prompt_out, comp_out)


def solution(mesh):
    placed = (
        P(),
        P(),
        P(),
        P(),
        P("seq", "samp"),
        P("samp"),
        P("samp", "seq"),
        P("seq", "samp"),
        P(None, "seq", None, None),
    )
    return jax.shard_map(
        body,
        mesh=mesh,
        in_specs=placed,
        out_specs=(P("seq", "samp"), P("seq", None, "samp")),
        check_vma=False,
    )
```

profile of v0, /device:TPU:6, one launch (start us, length us, event | category | flops | bytes accessed | tf_op | source)
XLA Modules:
  0.0 450.5 jit_solution(9055723753952659364)
XLA Ops:
  10.8 11.6 %gather_fusion = bf16[2176,512]{1,0:T(8,128)(2,1)S(1)} fusion(bf16[8016,512]{1,0:T(8,128)(2,1)} %param.15, s32[3072]{0:T(1024)S(1)} %pad_clamp_fusion), kind=kCustom, calls=%fused_computation | custom fusion | bytes 4465152 | tf_op jit(solution)/shard_map/jit(_take)/gather | solution.py:137
  22.4 2.8 select_select_fusion
  25.9 84.2 %all-reduce.2.cloned.1.call-done = bf16[2176,512]{1,0:T(8,128)(2,1)} async-done(((bf16[2176,512]{1,0:T(8,128)(2,1)}), bf16[2176,512]{1,0:T(8,128)(2,1)}) %all-reduce.2.cloned.1.call-update) | async-done | bytes 2228240 | tf_op jit(solution)/shard_map/psum | solution.py:139
  110.1 2.1 fusion.26
  113.0 6.9 %all-to-all-start = ((f32[16,1,2176]{2,1,0:T(1,128)}), f32[16,1,2176]{2,1,0:T(1,128)S(1)}, u32[]{:S(2)}, u32[]{:S(2)}) async-start(f32[16,1,2176]{2,1,0:T(1,128)} %broadcast_in_dim.154), calls=%async_computation | async-start | bytes 278528 | tf_op jit(solution)/shard_map/all_to_all | solution.py:13
  119.9 10.1 %all-to-all-done = f32[16,1,2176]{2,1,0:T(1,128)S(1)} async-done(((f32[16,1,2176]{2,1,0:T(1,128)}), f32[16,1,2176]{2,1,0:T(1,128)S(1)}, u32[]{:S(2)}, u32[]{:S(2)}) %all-to-all-start) | async-done | bytes 139296 | tf_op jit(solution)/shard_map/all_to_all | solution.py:13
  130.1 3.6 fusion.28
  133.7 3.7 all-to-all-start.1
  139.6 51.7 %all-to-all-done.1 = bf16[16,136,512]{2,1,0:T(8,128)(2,1)S(1)} async-done(((bf16[16,136,512]{2,1,0:T(8,128)(2,1)}), bf16[16,136,512]{2,1,0:T(8,128)(2,1)S(1)}, u32[]{:S(2)}, u32[]{:S(2)}) %all-to-all-start.1) | async-done | bytes 2228256 | tf_op jit(solution)/shard_map/all_to_all | solution.py:146
  191.3 2.1 copy.28
  193.5 3.6 reshape.686
  197.0 12.0 %all-gather.4.cloned.1.call-done = bf16[8192,1280]{1,0:T(8,128)(2,1)} async-done(((bf16[512,1280]{1,0:T(8,128)(2,1)}), bf16[8192,1280]{1,0:T(8,128)(2,1)}) %all-gather.4.cloned.1.call-update) | async-done | bytes 20971536 | tf_op jit(solution)/shard_map/all_gather | solution.py:149
  209.0 26.8 %copy.29 = bf16[1280,8192]{1,0:T(8,128)(2,1)} copy(bf16[1280,8192]{0,1:T(8,128)(2,1)} %bitcast.260) | data formatting | bytes 41943040 | tf_op jit(solution)/shard_map/dot_general | solution.py:147
  235.8 10.7 %fusion.83 = (bf16[136,1,10,128]{3,0,2,1:T(8,128)(2,1)S(1)}, f32[136,1,10,128]{3,0,2,1:T(8,128)S(1)}) fusion(bf16[136,8192,1]{1,0,2:T(8,128)(2,1)S(1)} %reshape.686, bf16[10,128,8192]{2,1,0:T(8,128)(2,1)} %bitcast.259), kind=kOutput, calls=%fused_computation.144 | convolution fusion | flops 2852300800 | bytes 24244224 | tf_op jit(solution)/shard_map/dot_general | solution.py:147
  250.5 80.6 %while.18 = (s32[]{:T(128)}, f32[136,1,8]{0,2,1:T(8,128)S(1)}, f32[136,1,8]{0,2,1:T(8,128)S(1)}, f32[136,1,8,128]{3,0,2,1:T(8,128)}, s32[]{:T(128)}, /*index=5*/...) while((s32[]{:T(128)}, f32[136,1,8]{0,2,1:T(8,128)S(1)}, ...), condition=%wide.region_6.7_spmd.clone, body=%wide.region_3.6_spmd.clone.sunk | while | flops 1170246016 | bytes 33724172 | solution.py:177
  251.2 2.6 bitcast_reduce_fusion.2
  253.9 2.3 fusion.95
  256.3 3.5 fusion.96
  261.3 2.6 bitcast_reduce_fusion.2
  264.0 2.3 fusion.95
  266.3 3.5 fusion.96
  271.4 2.6 bitcast_reduce_fusion.2
  274.0 2.3 fusion.95
  276.4 3.5 fusion.96
  281.4 2.7 bitcast_reduce_fusion.2
  284.1 2.3 fusion.95
  286.5 3.5 fusion.96
  291.5 2.6 bitcast_reduce_fusion.2
  294.2 2.3 fusion.95
  296.5 3.5 fusion.96
  301.6 2.6 bitcast_reduce_fusion.2
  304.2 2.3 fusion.95
  306.6 3.5 fusion.96
  311.6 2.6 bitcast_reduce_fusion.2
  314.3 2.3 fusion.95
  316.7 3.5 fusion.96
  321.7 2.6 bitcast_reduce_fusion.2
  324.4 2.3 fusion.95
  326.7 3.5 fusion.96
  331.5 2.9 fusion.23
  334.4 3.1 fusion.24
  338.7 2.4 fusion.46
  341.9 53.3 %all-gather.8.cloned.1.call-done = bf16[2176,1024]{1,0:T(8,128)(2,1)} async-done(((bf16[136,1024]{1,0:T(8,128)(2,1)}), bf16[2176,1024]{1,0:T(8,128)(2,1)}) %all-gather.8.cloned.1.call-update) | async-done | bytes 4456464 | tf_op jit(solution)/shard_map/all_gather | solution.py:204
  395.2 4.7 %convolution_convert_fusion = bf16[2176,512]{1,0:T(8,128)(2,1)S(1)} fusion(bf16[2176,1024]{1,0:T(8,128)(2,1)} %all-gather.8.cloned.1.call-done, bf16[1024,512]{1,0:T(8,128)(2,1)S(1)} %copy-done), kind=kOutput, calls=%fused_computation.37 | convolution fusion | flops 2282815488 | bytes 7733248 | tf_op jit(solution)/shard_map/dot_general | solution.py:203
  400.2 1.6 pad_maximum_fusion
  401.8 4.8 %all-to-all-start.2 = ((bf16[8,272,512]{2,1,0:T(8,128)(2,1)}), bf16[8,272,512]{2,1,0:T(8,128)(2,1)}, u32[]{:S(2)}, u32[]{:S(2)}) async-start(bf16[8,272,512]{2,1,0:T(8,128)(2,1)} %pad_maximum_fusion), calls=%async_computation.2 | async-start | bytes 4456448 | tf_op jit(solution)/shard_map/all_to_all | solution.py:37
  407.0 32.4 %all-to-all-done.2 = bf16[8,272,512]{2,1,0:T(8,128)(2,1)} async-done(((bf16[8,272,512]{2,1,0:T(8,128)(2,1)}), bf16[8,272,512]{2,1,0:T(8,128)(2,1)}, u32[]{:S(2)}, u32[]{:S(2)}) %all-to-all-start.2) | async-done | bytes 2228256 | tf_op jit(solution)/shard_map/all_to_all | solution.py:37
  439.5 2.0 convert_reduce_fusion
  (139 shorter events, 25.8 us)
Async XLA Ops:
  8.0 387.2 %copy-start = (bf16[1024,512]{1,0:T(8,128)(2,1)S(1)}, bf16[1024,512]{1,0:T(8,128)(2,1)}, u32[]{:S(2)}) copy-start(bf16[1024,512]{1,0:T(8,128)(2,1)} %param.18) | copy-start | bytes 3145732
  8.0 102.1 %all-reduce.2.cloned.1.call-start = ((), (), s32[]{:S(2)}) async-start(), calls=%async_computation.3 | async-start | bytes 4456448 | tf_op jit(solution)/shard_map/psum | solution.py:139
  22.4 97.4 %copy-start.8 = (bf16[512]{0:T(512)(128)(2,1)S(1)}, bf16[512]{0:T(512)(128)(2,1)}, u32[]{:S(2)}) copy-start(bf16[512]{0:T(512)(128)(2,1)} %param.16) | copy-start | bytes 3076
  25.3 183.7 %all-gather.4.cloned.1.call-start = ((), (), s32[]{:S(2)}) async-start(), calls=%async_computation.4 | async-start | bytes 22282240 | tf_op jit(solution)/shard_map/all_gather | solution.py:149
  113.0 17.0 %all-to-all-start = ((f32[16,1,2176]{2,1,0:T(1,128)}), f32[16,1,2176]{2,1,0:T(1,128)S(1)}, u32[]{:S(2)}, u32[]{:S(2)}) async-start(f32[16,1,2176]{2,1,0:T(1,128)} %broadcast_in_dim.154), calls=%async_computation | async-start | bytes 278528 | tf_op jit(solution)/shard_map/all_to_all | solution.py:13
  133.7 57.7 %all-to-all-start.1 = ((bf16[16,136,512]{2,1,0:T(8,128)(2,1)}), bf16[16,136,512]{2,1,0:T(8,128)(2,1)S(1)}, u32[]{:S(2)}, u32[]{:S(2)}) async-start(bf16[16,136,512]{2,1,0:T(8,128)(2,1)} %bitcast.264), calls=%async_computation.1 | async-start | bytes 4456448 | tf_op jit(solution)/shard_map/all_to_all | solution.py:146
  137.4 194.1 %all-gather.6.cloned.1.call-start = ((), (), s32[]{:S(2)}) async-start(), calls=%async_computation.5 | async-start | bytes 1114112 | tf_op jit(solution)/shard_map/all_gather | solution.py:22
  246.6 0.7 copy-start.4
  246.6 1.0 copy-start.2
  248.6 146.6 %all-gather.8.cloned.1.call-start = ((), (), s32[]{:S(2)}) async-start(), calls=%async_computation.6 | async-start | bytes 4734976 | tf_op jit(solution)/shard_map/all_gather | solution.py:204
  250.5 81.0 %copy-start.3 = (pred[136,2048]{1,0:T(8,128)(4,1)S(1)}, pred[136,2048]{1,0:T(8,128)(4,1)}, u32[]{:S(2)}) copy-start(pred[136,2048]{1,0:T(8,128)(4,1)} %iota_compare_fusion) | copy-start | bytes 835588
  253.9 2.4 copy-start.5
  259.8 0.8 copy-start.6
  264.0 2.4 copy-start.5
  269.9 0.8 copy-start.6
  274.0 2.4 copy-start.5
  279.9 0.8 copy-start.6
  284.1 2.4 copy-start.5
  290.0 0.8 copy-start.6
  294.2 2.4 copy-start.5
  300.1 0.8 copy-start.6
  304.2 2.4 copy-start.5
  310.1 0.8 copy-start.6
  314.3 2.4 copy-start.5
  320.2 0.8 copy-start.6
  324.4 2.4 copy-start.5
  330.3 0.8 copy-start.6
  334.4 3.2 copy-start.7
  334.4 4.3 copy-start.9
  400.2 6.4 %copy-start.1 = (bf16[2176,512]{1,0:T(8,128)(2,1)S(1)}, bf16[2176,512]{1,0:T(8,128)(2,1)}, u32[]{:S(2)}) copy-start(bf16[2176,512]{1,0:T(8,128)(2,1)} %all-reduce.2.cloned.1.call-done) | copy-start | bytes 6684676
  401.8 37.7 %all-to-all-start.2 = ((bf16[8,272,512]{2,1,0:T(8,128)(2,1)}), bf16[8,272,512]{2,1,0:T(8,128)(2,1)}, u32[]{:S(2)}, u32[]{:S(2)}) async-start(bf16[8,272,512]{2,1,0:T(8,128)(2,1)} %pad_maximum_fusion), calls=%async_computation.2 | async-start | bytes 4456448 | tf_op jit(solution)/shard_map/all_to_all | solution.py:37
Sparse Core Ops, SparseCore 0:
  25.4 84.6 all-reduce.1
Sparse Core Ops, SparseCore 1:
  28.3 180.7 all-gather.3
  248.7 42.1 all-gather.5
  342.0 53.1 all-gather.7
where the time goes:
time: 453 us; the launch traced here: 451 us
  waiting for transfers between devices  244 us (54%)
  matrix products  71.7 us (16%)
  local copies, waits for them, and re-layouts  56.1 us (12%)
  other arithmetic  45.4 us (10%)
  between operations  16.7 us (4%)
  starting transfers between devices  15.7 us (3%)
    psum x1, waiting for transfers between devices, body(): lax.psum(partial_rows, 'seq').astype(jnp.float32).astype(jnp.bfloat16)  84.2 us
    all_gather x1, waiting for transfers between devices, body(): lax.all_gather(context, 'samp', axis=0, tiled=True)  53.3 us
    all_to_all x1, waiting for transfers between devices, body(): lax.all_to_all(normalized_rows, 'samp', split_axis=0, concat_axis=1, tile...  51.7 us
    all_to_all x1, waiting for transfers between devices, sent_and_summed(): lax.all_to_all(in_blocks(shard, dim, length), axis, 0, 0, tiled=True)  32.4 us
    dot_general x10, matrix products, absorb(): jnp.einsum('rgqk,' + key_form + '->rgqd', weights.astype(jnp.bfloat16), v...  31.8 us
    dot_general x1, local copies, waits for them, and re-layouts, body(): jnp.dot(own_features, lax.all_gather(query_key_value_weight, 'samp', axis...  26.8 us
    dot_general x10, matrix products, absorb(): jnp.einsum('rgqd,' + key_form + '->rgqk', queries, key_block, preferred_e...  24.4 us
    reduce_sum x10, other arithmetic, absorb(): run_sum = run_sum * factor + jnp.sum(weights, axis=-1)  21.9 us
  transfers between devices with their start and end apart: 7, of which 6 were waited for; matrix products, arithmetic and copies ran while one was open for 20% of the time, Pallas kernels for 0%

commit v1 on v0

--- a/solution.py
+++ b/solution.py
@@ -6,6 +6,11 @@
 
 NORM_EPS = 1e-05
 MASK_FILL = -1e30
+
+
+def add_all(value, axis):
+    terms = lax.all_gather(value, axis)
+    return jnp.sum(terms, axis=0)
 
 
 def from_everyone(shard, axis):
@@ -136,7 +141,7 @@
     inside = (local_ids >= 0) & (local_ids < vocab_rows)
     picked = jnp.take(embed_table, jnp.clip(local_ids, 0, vocab_rows - 1), axis=0)
     partial_rows = jnp.where(inside[:, None], picked, jnp.zeros((), jnp.bfloat16))
-    embedded = lax.psum(partial_rows, "seq").astype(jnp.float32).astype(jnp.bfloat16)
+    embedded = add_all(partial_rows, "seq").astype(jnp.float32).astype(jnp.bfloat16)
     wide = embedded.astype(jnp.float32)
     square_sums = of_everyone(jnp.sum(wide * wide, axis=1), "samp")
     inv_rms = lax.rsqrt(square_sums / (local_width * samp_count) + NORM_EPS)

time: 453 us -> 607 us (1.34)
  waiting for transfers between devices: 244 us -> 387 us
  other arithmetic: 45.4 us -> 52.3 us
    all_gather x0 -> x1, waiting for transfers between devices: none -> 180 us  [add_all(): terms = lax.all_gather(value, axis)]
    psum x1 -> x0, waiting for transfers between devices: 84.2 us -> none  [body(): lax.psum(partial_rows, 'seq').astype(jnp.float32).astype(jnp.bfloat16)]
    all_gather x1, waiting for transfers between devices: 12 us -> 76.8 us  [body(): lax.all_gather(query_key_value_weight, 'samp', axis=0, tiled=True)]
    all_to_all x1, waiting for transfers between devices: 51.7 us -> 33.8 us  [body(): lax.all_to_all(normalized_rows, 'samp', split_axis=0, concat_axis=1, tile...]
    reduce_sum x0 -> x1, other arithmetic: none -> 9.52 us  [add_all(): return jnp.sum(terms, axis=0)]
  transfers between devices with their start and end apart: 7 -> 7, of which waited for: 6 -> 6; matrix products, arithmetic and copies ran while one was open for 20% -> 17% of each run, Pallas kernels for 0% -> 0%
where the time goes in v1:
time: 607 us; the launch traced here: 605 us
  waiting for transfers between devices  387 us (64%)
  matrix products  73.7 us (12%)
  local copies, waits for them, and re-layouts  60.1 us (10%)
  other arithmetic  52.3 us (9%)
  starting transfers between devices  16.3 us (3%)
  between operations  14.9 us (2%)
    all_gather x1, waiting for transfers between devices, add_all(): terms = lax.all_gather(value, axis)  180 us
    all_gather x1, waiting for transfers between devices, body(): lax.all_gather(query_key_value_weight, 'samp', axis=0, tiled=True)  76.8 us
    all_gather x1, waiting for transfers between devices, body(): lax.all_gather(context, 'samp', axis=0, tiled=True)  53.6 us
    all_to_all x1, waiting for transfers between devices, body(): lax.all_to_all(normalized_rows, 'samp', split_axis=0, concat_axis=1, tile...  33.8 us
    all_to_all x1, waiting for transfers between devices, sent_and_summed(): lax.all_to_all(in_blocks(shard, dim, length), axis, 0, 0, tiled=True)  32.5 us
    dot_general x10, matrix products, absorb(): jnp.einsum('rgqk,' + key_form + '->rgqd', weights.astype(jnp.bfloat16), v...  31.8 us
    dot_general x1, local copies, waits for them, and re-layouts, body(): jnp.dot(own_features, lax.all_gather(query_key_value_weight, 'samp', axis...  26.8 us
    dot_general x10, matrix products, absorb(): jnp.einsum('rgqd,' + key_form + '->rgqk', queries, key_block, preferred_e...  25.7 us
  transfers between devices with their start and end apart: 7, of which 6 were waited for; matrix products, arithmetic and copies ran while one was open for 17% of the time, Pallas kernels for 0%

profile of v1, /device:TPU:6, one launch (start us, length us, event | category | flops | bytes accessed | tf_op | source)
XLA Modules:
  0.0 605.3 jit_solution(16725234878786681303)
XLA Ops:
  10.0 11.6 %gather_fusion = bf16[2176,512]{1,0:T(8,128)(2,1)S(1)} fusion(bf16[8016,512]{1,0:T(8,128)(2,1)} %param.15, s32[3072]{0:T(1024)S(1)} %pad_clamp_fusion), kind=kCustom, calls=%fused_computation | custom fusion | bytes 4465152 | tf_op jit(solution)/shard_map/jit(_take)/gather | solution.py:142
  21.6 2.8 fusion.30
  25.2 179.8 %all-gather.5.cloned.1.call-done = bf16[8,2176,512]{2,1,0:T(8,128)(2,1)} async-done(((bf16[1,2176,512]{2,1,0:T(8,128)(2,1)}), bf16[8,2176,512]{2,1,0:T(8,128)(2,1)}) %all-gather.5.cloned.1.call-update) | async-done | bytes 17825808 | tf_op jit(solution)/shard_map/all_gather | solution.py:12
  205.0 9.5 %reduce_sum.76 = bf16[2176,512]{1,0:T(8,128)(2,1)S(1)} reduce(bf16[8,2176,512]{2,1,0:T(8,128)(2,1)} %all-gather.5.cloned.1.call-done, bf16[]{:T(256)} %constant.170.clone.1), dimensions={0}, to_apply=%region_0.1 | reduce | flops 7798784 | bytes 20054018 | tf_op jit(solution)/shard_map/reduce_sum | solution.py:13
  215.8 6.7 %all-to-all-start = ((f32[16,1,2176]{2,1,0:T(1,128)}), f32[16,1,2176]{2,1,0:T(1,128)S(1)}, u32[]{:S(2)}, u32[]{:S(2)}) async-start(f32[16,1,2176]{2,1,0:T(1,128)} %broadcast_in_dim.154), calls=%async_computation | async-start | bytes 278528 | tf_op jit(solution)/shard_map/all_to_all | solution.py:18
  222.5 10.1 %all-to-all-done = f32[16,1,2176]{2,1,0:T(1,128)S(1)} async-done(((f32[16,1,2176]{2,1,0:T(1,128)}), f32[16,1,2176]{2,1,0:T(1,128)S(1)}, u32[]{:S(2)}, u32[]{:S(2)}) %all-to-all-start) | async-done | bytes 139296 | tf_op jit(solution)/shard_map/all_to_all | solution.py:18
  232.8 2.0 multiply_convert_fusion
  234.8 4.4 all-to-all-start.1
  242.0 33.8 %all-to-all-done.1 = bf16[16,136,512]{2,1,0:T(8,128)(2,1)} async-done(((bf16[16,136,512]{2,1,0:T(8,128)(2,1)}), bf16[16,136,512]{2,1,0:T(8,128)(2,1)}, u32[]{:S(2)}, u32[]{:S(2)}) %all-to-all-start.1) | async-done | bytes 2228256 | tf_op jit(solution)/shard_map/all_to_all | solution.py:151
  275.8 3.8 copy.27
  279.6 4.8 reshape.745
  284.4 76.8 %all-gather.7.cloned.1.call-done = bf16[8192,1280]{1,0:T(8,128)(2,1)} async-done(((bf16[512,1280]{1,0:T(8,128)(2,1)}), bf16[8192,1280]{1,0:T(8,128)(2,1)}) %all-gather.7.cloned.1.call-update) | async-done | bytes 20971536 | tf_op jit(solution)/shard_map/all_gather | solution.py:154
  361.1 26.8 %copy.28 = bf16[1280,8192]{1,0:T(8,128)(2,1)} copy(bf16[1280,8192]{0,1:T(8,128)(2,1)} %bitcast.266) | data formatting | bytes 41943040 | tf_op jit(solution)/shard_map/dot_general | solution.py:152
  387.9 11.4 %fusion.81 = (bf16[136,1,10,128]{3,0,2,1:T(8,128)(2,1)S(1)}, f32[136,1,10,128]{3,0,2,1:T(8,128)S(1)}) fusion(bf16[136,8192,1]{1,0,2:T(8,128)(2,1)} %reshape.745, bf16[10,128,8192]{2,1,0:T(8,128)(2,1)} %bitcast.262), kind=kOutput, calls=%fused_computation.142 | convolution fusion | flops 2852300800 | bytes 24244224 | tf_op jit(solution)/shard_map/dot_general | solution.py:152
  404.5 80.7 %while.18 = (s32[]{:T(128)}, f32[136,1,8]{0,2,1:T(8,128)}, f32[136,1,8]{0,2,1:T(8,128)}, f32[136,1,8,128]{3,0,2,1:T(8,128)}, s32[]{:T(128)}, /*index=5*/bf16[2,1...) while((s32[]{:T(128)}, f32[136,1,8]{0,2,1:T(8,128)}, ...), condition=%wide.region_6.7_spmd.clone, body=%wide.region_3.6_spmd.clone.sunk | while | flops 1170246016 | bytes 33776480 | solution.py:182
  405.2 2.7 bitcast_reduce_fusion.2
  407.9 2.3 fusion.93
  410.3 3.5 fusion.94
  415.3 2.6 bitcast_reduce_fusion.2
  418.0 2.3 fusion.93
  420.4 3.5 fusion.94
  425.4 2.6 bitcast_reduce_fusion.2
  428.1 2.3 fusion.93
  430.4 3.5 fusion.94
  435.5 2.7 bitcast_reduce_fusion.2
  438.1 2.3 fusion.93
  440.5 3.5 fusion.94
  445.5 2.6 bitcast_reduce_fusion.2
  448.2 2.3 fusion.93
  450.6 3.5 fusion.94
  455.6 2.6 bitcast_reduce_fusion.2
  458.3 2.3 fusion.93
  460.7 3.5 fusion.94
  465.7 2.6 bitcast_reduce_fusion.2
  468.4 2.3 fusion.93
  470.8 3.5 fusion.94
  475.8 2.6 bitcast_reduce_fusion.2
  478.5 2.3 fusion.93
  480.8 3.5 fusion.94
  486.6 3.2 fusion.23
  489.9 3.1 fusion.24
  494.2 2.4 fusion.44
  497.4 53.6 %all-gather.11.cloned.1.call-done = bf16[2176,1024]{1,0:T(8,128)(2,1)} async-done(((bf16[136,1024]{1,0:T(8,128)(2,1)}), bf16[2176,1024]{1,0:T(8,128)(2,1)}) %all-gather.11.cloned.1.call-update) | async-done | bytes 4456464 | tf_op jit(solution)/shard_map/all_gather | solution.py:209
  551.1 4.7 convolution_convert_fusion
  556.0 1.6 pad_maximum_fusion
  557.6 4.8 all-to-all-start.2
  562.8 32.5 %all-to-all-done.2 = bf16[8,272,512]{2,1,0:T(8,128)(2,1)} async-done(((bf16[8,272,512]{2,1,0:T(8,128)(2,1)}), bf16[8,272,512]{2,1,0:T(8,128)(2,1)}, u32[]{:S(2)}, u32[]{:S(2)}) %all-to-all-start.2) | async-done | bytes 2228256 | tf_op jit(solution)/shard_map/all_to_all | solution.py:42
  595.3 2.0 convert_reduce_fusion
  (201 shorter events, 29.2 us)
Async XLA Ops:
  7.2 543.9 %copy-start = (bf16[1024,512]{1,0:T(8,128)(2,1)S(1)}, bf16[1024,512]{1,0:T(8,128)(2,1)}, u32[]{:S(2)}) copy-start(bf16[1024,512]{1,0:T(8,128)(2,1)} %param.18) | copy-start | bytes 3145732
  7.2 197.8 %all-gather.5.cloned.1.call-start = ((), (), s32[]{:S(2)}) async-start(), calls=%async_computation.3 | async-start | bytes 20054016 | tf_op jit(solution)/shard_map/all_gather | solution.py:12
  24.4 336.7 %all-gather.7.cloned.1.call-start = ((), (), s32[]{:S(2)}) async-start(), calls=%async_computation.4 | async-start | bytes 22282240 | tf_op jit(solution)/shard_map/all_gather | solution.py:154
  25.2 197.3 %copy-start.17 = (bf16[512]{0:T(512)(128)(2,1)S(1)}, bf16[512]{0:T(512)(128)(2,1)}, u32[]{:S(2)}) copy-start(bf16[512]{0:T(512)(128)(2,1)} %param.16) | copy-start | bytes 3076
  215.8 16.8 %all-to-all-start = ((f32[16,1,2176]{2,1,0:T(1,128)}), f32[16,1,2176]{2,1,0:T(1,128)S(1)}, u32[]{:S(2)}, u32[]{:S(2)}) async-start(f32[16,1,2176]{2,1,0:T(1,128)} %broadcast_in_dim.154), calls=%async_computation | async-start | bytes 278528 | tf_op jit(solution)/shard_map/all_to_all | solution.py:18
  234.8 41.0 %all-to-all-start.1 = ((bf16[16,136,512]{2,1,0:T(8,128)(2,1)}), bf16[16,136,512]{2,1,0:T(8,128)(2,1)}, u32[]{:S(2)}, u32[]{:S(2)}) async-start(bf16[16,136,512]{2,1,0:T(8,128)(2,1)} %multiply_convert_fusion), calls=%async_computation.1 | async-start | bytes 4456448 | tf_op jit(solution)/shard_map/all_to_all | solution.py:151
  239.3 247.4 %all-gather.9.cloned.1.call-start = ((), (), s32[]{:S(2)}) async-start(), calls=%async_computation.5 | async-start | bytes 1114112 | tf_op jit(solution)/shard_map/all_gather | solution.py:27
  399.3 0.9 copy-start.1
  399.3 1.2 copy-start.7
  401.9 149.1 %all-gather.11.cloned.1.call-start = ((), (), s32[]{:S(2)}) async-start(), calls=%async_computation.6 | async-start | bytes 4734976 | tf_op jit(solution)/shard_map/all_gather | solution.py:209
  403.7 0.9 copy-start.3
  405.2 2.7 copy-start.4
  407.9 2.4 copy-start.8
  410.3 3.6 copy-start.13
  413.8 0.8 copy-start.9
  415.3 2.7 copy-start.4
  418.0 2.4 copy-start.8
  420.3 3.6 copy-start.13
  423.9 0.8 copy-start.9
  425.4 2.7 copy-start.4
  428.1 2.4 copy-start.8
  430.4 3.5 copy-start.13
  434.0 0.8 copy-start.9
  435.4 2.7 copy-start.4
  438.1 2.4 copy-start.8
  440.5 3.6 copy-start.13
  444.1 0.8 copy-start.9
  445.5 2.7 copy-start.4
  448.2 2.4 copy-start.8
  450.6 3.6 copy-start.13
  454.2 0.8 copy-start.9
  455.6 2.7 copy-start.4
  458.3 2.4 copy-start.8
  460.7 3.5 copy-start.13
  464.2 0.8 copy-start.9
  465.7 2.7 copy-start.4
  468.4 2.4 copy-start.8
  470.8 3.5 copy-start.13
  475.8 2.7 copy-start.4
  478.5 2.4 copy-start.8
  480.8 3.5 copy-start.13
  486.6 3.2 copy-start.5
  486.6 3.2 copy-start.6
  489.8 3.1 copy-start.16
  489.8 3.2 copy-start.15
  489.9 3.2 copy-start.10
  489.9 4.3 copy-start.18
  557.6 37.7 %all-to-all-start.2 = ((bf16[8,272,512]{2,1,0:T(8,128)(2,1)}), bf16[8,272,512]{2,1,0:T(8,128)(2,1)}, u32[]{:S(2)}, u32[]{:S(2)}) async-start(bf16[8,272,512]{2,1,0:T(8,128)(2,1)} %pad_maximum_fusion), calls=%async_computation.2 | async-start | bytes 4456448 | tf_op jit(solution)/shard_map/all_to_all | solution.py:42
  (13 other events, 9.7 us)
Sparse Core Ops, SparseCore 0:
  24.5 180.4 all-gather.4
  207.5 153.5 all-gather.6
  402.0 42.3 all-gather.8
  497.5 53.4 all-gather.10
